TPU v7x, 32 devices: a whole 2x2x4 slice. The times are simulated.
32 devices in a mesh: ctx: 8 (over z, y), fsdp: 4 (over x, core).
Axes of the slice: x: 2, y: 2, z: 4, core: 2. Of those that a mesh axis runs over, the one named last changes fastest.
Arguments:
- tokens: bfloat16 [4, 2048, 1024], P('fsdp', 'ctx'), may hold values from -6 to 6
- out_grad: bfloat16 [4, 2048, 1024], P('fsdp', 'ctx'), may hold values from -6 to 6
- lengths: int32 [4, 1], P('fsdp'), may hold values from 512 to 2048, as said below
- norm1_gain: bfloat16 [1024], P('fsdp'), may hold values from 0.5 to 1.5
- w_query: bfloat16 [1024, 1024], P('fsdp'), may hold values from -0.1875 to 0.1875
- w_latent: bfloat16 [1024, 512], P('fsdp'), may hold values from -0.1875 to 0.1875
- w_key_up: bfloat16 [1024, 256], P('fsdp'), may hold values from -0.75 to 0.75
- w_value_up: bfloat16 [1024, 256], P('fsdp'), may hold values from -0.375 to 0.375
- w_output: bfloat16 [1024, 1024], P('fsdp'), may hold values from -1.5 to 1.5
- norm2_gain: bfloat16 [1024], P('fsdp'), may hold values from 0.5 to 1.5
- w_gate: bfloat16 [1024, 2816], P(None, 'fsdp'), may hold values from -0.1875 to 0.1875
- w_up: bfloat16 [1024, 2816], P(None, 'fsdp'), may hold values from -0.1875 to 0.1875
- w_down: bfloat16 [2816, 1024], P('fsdp'), may hold values from -0.109375 to 0.109375
Outputs:
- result: bfloat16 [4, 2048, 1024], P('fsdp', 'ctx')
- token_grad: float32 [4, 2048, 1024], P('fsdp', 'ctx')
- norm1_gain_grad: float32 [1024], P('fsdp')
- w_query_grad: float32 [1024, 1024], P('fsdp')
- w_latent_grad: float32 [1024, 512], P('fsdp')
- w_key_up_grad: float32 [1024, 256], P('fsdp')
- w_value_up_grad: float32 [1024, 256], P('fsdp')
- w_output_grad: float32 [1024, 1024], P('fsdp')
- norm2_gain_grad: float32 [1024], P('fsdp')
- w_gate_grad: float32 [1024, 2816], P(None, 'fsdp')
- w_up_grad: float32 [1024, 2816], P(None, 'fsdp')
- w_down_grad: float32 [2816, 1024], P('fsdp')
Inputs may be any that keep to these rules, and one draw needn't show every extreme that they name: lengths[g, j] valid tokens stand at the start of slot j of group g; the rest of the slot of 2048 rows is padding.
All inputs are finite; a program needn't handle non-finite values.
Results may differ from a plain program's by a relative error of at most 0.025.
Values may be sent and summed in bfloat16 or wider, within the bound.
No kernel may reach another device: no remote copies, remote signals or barrier semaphores. Data moves between devices by JAX's collectives and lax.ppermute only.
A program may use at most 192 MiB of HBM per device.

v0:
```python
import jax
import jax.numpy as jnp
from jax import lax
from jax.sharding import PartitionSpec as P

NH = 16
HD = 64
LAT = 256
GRP = 2
SEQ_MAX = 4096
EPS = 1e-06
NEGATIVE = -1e30


def norm_scale(values):
    return lax.rsqrt(jnp.mean(values * values, axis=-1, keepdims=True) + EPS)


def norm_back(grad_in, normed, scale_rows, gain_full):
    scaled = grad_in * gain_full
    return scale_rows * (scaled - normed * jnp.mean(scaled * normed, axis=-1, keepdims=True))


def key_mask(key_start, key_rows, slot_start, query_pos, length):
    relative = key_start - slot_start + jnp.arange(key_rows, dtype=jnp.int32)
    return (
        (relative[None, :] >= 0)
        & (relative[None, :] <= query_pos[:, None])
        & (relative[None, :] < length)
    )


def raw_scores(query_groups, key_piece, allowed, score_scale):
    grouped = key_piece.reshape(key_piece.shape[0], GRP, LAT)
    scores = (
        jnp.einsum("gpql,kgl->gpqk", query_groups, grouped, preferred_element_type=jnp.float32)
        * score_scale
    )
    return (jnp.where(allowed[None, None], scores, NEGATIVE), grouped)


def on_device(
    tokens,
    out_grad,
    lengths,
    norm1_gain,
    w_query,
    w_latent,
    w_key_up,
    w_value_up,
    w_output,
    norm2_gain,
    w_gate,
    w_up,
    w_down,
):
    ctx_size = lax.axis_size("ctx")
    tok_rows = tokens.shape[1]
    group_rows = tok_rows * ctx_size
    seq_rows = min(SEQ_MAX, group_rows)
    slot_blocks = seq_rows // tok_rows
    head_groups = NH // GRP
    lat_width = GRP * LAT
    my_start = lax.axis_index("ctx") * tok_rows
    slot_number = my_start // seq_rows
    slot_start = slot_number * seq_rows
    length = jnp.sum(
        jnp.where(jnp.arange(lengths.shape[1], dtype=jnp.int32) == slot_number, lengths[0], 0)
    )
    query_pos = my_start - slot_start + jnp.arange(tok_rows, dtype=jnp.int32)
    row_valid = (query_pos < length).astype(jnp.float32)[:, None]
    score_scale = HD ** (-0.5)
    gain_one, query_full, latent_full, key_full, value_full, output_full = (
        lax.all_gather(norm1_gain, "fsdp", axis=0, tiled=True),
        lax.all_gather(w_query, "fsdp", axis=0, tiled=True),
        lax.all_gather(w_latent, "fsdp", axis=0, tiled=True),
        lax.all_gather(w_key_up, "fsdp", axis=0, tiled=True),
        lax.all_gather(w_value_up, "fsdp", axis=0, tiled=True),
        lax.all_gather(w_output, "fsdp", axis=0, tiled=True),
    )
    gain_two, gate_full, up_full, down_full = (
        lax.all_gather(norm2_gain, "fsdp", axis=0, tiled=True),
        lax.all_gather(w_gate, "fsdp", axis=1, tiled=True),
        lax.all_gather(w_up, "fsdp", axis=1, tiled=True),
        lax.all_gather(w_down, "fsdp", axis=0, tiled=True),
    )
    gain_one_f = gain_one.astype(jnp.float32)
    gain_two_f = gain_two.astype(jnp.float32)
    inputs = tokens[0].astype(jnp.float32)
    scale_one = norm_scale(inputs)
    normed_one = inputs * scale_one
    normed = (normed_one * gain_one_f).astype(jnp.bfloat16)
    queries = jnp.dot(normed, query_full, preferred_element_type=jnp.float32).astype(jnp.bfloat16)
    latent = jnp.dot(normed, latent_full, preferred_element_type=jnp.float32).astype(jnp.bfloat16)
    key_heads = key_full.reshape(NH, HD, LAT)
    query_latent = jnp.einsum(
        "shd,hdl->hsl",
        queries.reshape(tok_rows, NH, HD),
        key_heads,
        preferred_element_type=jnp.float32,
    ).astype(jnp.bfloat16)
    query_groups = query_latent.reshape(GRP, head_groups, tok_rows, LAT)

    def is_needed(key_start, key_rows):
        return (
            (key_start + key_rows > slot_start)
            & (key_start < slot_start + length)
            & (key_start < my_start + tok_rows)
        )

    def forward_update(state_now, key_piece, key_start):
        best_now, weight_sum, accum_now = state_now
        allowed = key_mask(key_start, key_piece.shape[0], slot_start, query_pos, length)
        scores, grouped = raw_scores(query_groups, key_piece, allowed, score_scale)
        best_next = jnp.maximum(best_now, jnp.max(scores, axis=-1))
        factor = jnp.exp(best_now - best_next)
        weights = jnp.where(allowed[None, None], jnp.exp(scores - best_next[..., None]), 0.0)
        weight_sum = weight_sum * factor + jnp.sum(weights, axis=-1)
        accum_now = accum_now * factor[..., None] + jnp.einsum(
            "gpqk,kgl->gpql",
            weights.astype(jnp.bfloat16),
            grouped,
            preferred_element_type=jnp.float32,
        )
        return (best_next, weight_sum, accum_now)

    def guarded_forward(state_now, key_piece, key_start):
        return lax.cond(
            is_needed(key_start, key_piece.shape[0]),
            lambda state_in: forward_update(state_in, key_piece, key_start),
            lambda state_in: state_in,
            state_now,
        )

    start_state = (
        jnp.full((GRP, head_groups, tok_rows), NEGATIVE, jnp.float32),
        jnp.zeros((GRP, head_groups, tok_rows), jnp.float32),
        jnp.zeros((GRP, head_groups, tok_rows, LAT), jnp.float32),
    )
    group_latent = lax.all_gather(latent, "ctx", axis=0, tiled=True)

    def forward_loop(block_index, state_now):
        key_start = slot_start + block_index * tok_rows
        key_piece = lax.dynamic_slice_in_dim(group_latent, key_start, tok_rows, 0)
        return guarded_forward(state_now, key_piece, key_start)

    final_state = lax.fori_loop(0, slot_blocks, forward_loop, start_state)
    best_final, sum_final, accum_final = final_state
    log_total = best_final + jnp.log(sum_final)
    mixture = accum_final / sum_final[..., None]
    mixture_low = mixture.astype(jnp.bfloat16)
    value_heads = value_full.reshape(NH, HD, LAT)
    attended = (
        jnp.einsum(
            "hsl,hdl->shd",
            mixture_low.reshape(NH, tok_rows, LAT),
            value_heads,
            preferred_element_type=jnp.float32,
        )
        .reshape(tok_rows, NH * HD)
        .astype(jnp.bfloat16)
    )
    branch = jnp.dot(attended, output_full, preferred_element_type=jnp.float32)
    middle = inputs + branch
    scale_two = norm_scale(middle)
    normed_two_raw = middle * scale_two
    normed_two = (normed_two_raw * gain_two_f).astype(jnp.bfloat16)
    gate_value = jnp.dot(normed_two, gate_full, preferred_element_type=jnp.float32)
    upward = jnp.dot(normed_two, up_full, preferred_element_type=jnp.float32)
    sigmoid_gate = jax.nn.sigmoid(gate_value)
    silu_gate = gate_value * sigmoid_gate
    hidden = (silu_gate * upward).astype(jnp.bfloat16)
    feed_out = jnp.dot(hidden, down_full, preferred_element_type=jnp.float32)
    result = ((middle + feed_out) * row_valid).astype(jnp.bfloat16)
    cotangent = out_grad[0].astype(jnp.float32) * row_valid
    feed_grad = cotangent.astype(jnp.bfloat16)
    down_grad = jnp.einsum("tf,td->fd", hidden, feed_grad, preferred_element_type=jnp.float32)
    hidden_grad = jnp.einsum("td,fd->tf", feed_grad, down_full, preferred_element_type=jnp.float32)
    gate_grad = (
        hidden_grad * upward * sigmoid_gate * (1.0 + gate_value * (1.0 - sigmoid_gate))
    ).astype(jnp.bfloat16)
    up_grad_in = (hidden_grad * silu_gate).astype(jnp.bfloat16)
    gate_w_grad = jnp.einsum("td,tf->df", normed_two, gate_grad, preferred_element_type=jnp.float32)
    up_w_grad = jnp.einsum("td,tf->df", normed_two, up_grad_in, preferred_element_type=jnp.float32)
    normed_two_grad = jnp.einsum(
        "tf,df->td", gate_grad, gate_full, preferred_element_type=jnp.float32
    ) + jnp.einsum("tf,df->td", up_grad_in, up_full, preferred_element_type=jnp.float32)
    gain_two_grad = jnp.sum(normed_two_grad * normed_two_raw, axis=0)
    middle_grad = cotangent + norm_back(normed_two_grad, normed_two_raw, scale_two, gain_two_f)
    branch_grad = middle_grad.astype(jnp.bfloat16)
    output_grad = jnp.einsum("tk,td->kd", attended, branch_grad, preferred_element_type=jnp.float32)
    attended_grad = jnp.einsum(
        "td,kd->tk", branch_grad, output_full, preferred_element_type=jnp.float32
    ).astype(jnp.bfloat16)
    attended_heads = attended_grad.reshape(tok_rows, NH, HD)
    value_grad = jnp.einsum(
        "shd,hsl->hdl",
        attended_heads,
        mixture_low.reshape(NH, tok_rows, LAT),
        preferred_element_type=jnp.float32,
    ).reshape(NH * HD, LAT)
    mixture_grad = (
        jnp.einsum("shd,hdl->hsl", attended_heads, value_heads, preferred_element_type=jnp.float32)
        .astype(jnp.bfloat16)
        .reshape(GRP, head_groups, tok_rows, LAT)
    )
    delta_sum = jnp.sum(mixture_grad * mixture, axis=-1)

    def back_term(query_grad_sum, key_piece, key_start):

        def compute(sum_in):
            allowed = key_mask(key_start, tok_rows, slot_start, query_pos, length)
            scores, grouped = raw_scores(query_groups, key_piece, allowed, score_scale)
            probs = jnp.where(allowed[None, None], jnp.exp(scores - log_total[..., None]), 0.0)
            probs_low = probs.astype(jnp.bfloat16)
            prob_grad = jnp.einsum(
                "gpql,kgl->gpqk", mixture_grad, grouped, preferred_element_type=jnp.float32
            )
            score_grad = (probs * (prob_grad - delta_sum[..., None])).astype(jnp.bfloat16)
            sum_out = sum_in + score_scale * jnp.einsum(
                "gpqk,kgl->gpql", score_grad, grouped, preferred_element_type=jnp.float32
            )
            key_term = score_scale * jnp.einsum(
                "gpqk,gpql->kgl", score_grad, query_groups, preferred_element_type=jnp.float32
            ) + jnp.einsum(
                "gpqk,gpql->kgl", probs_low, mixture_grad, preferred_element_type=jnp.float32
            )
            return (sum_out, key_term.reshape(tok_rows, lat_width))

        def skipped(sum_in):
            return (sum_in, jnp.zeros((tok_rows, lat_width), jnp.float32))

        return lax.cond(is_needed(key_start, tok_rows), compute, skipped, query_grad_sum)

    zero_query = jnp.zeros((GRP, head_groups, tok_rows, LAT), jnp.float32)

    def backward_loop(block_index, state_now):
        sum_now, key_grads = state_now
        key_start = slot_start + block_index * tok_rows
        key_piece = lax.dynamic_slice_in_dim(group_latent, key_start, tok_rows, 0)
        sum_now, key_term = back_term(sum_now, key_piece, key_start)
        key_grads = lax.dynamic_update_slice_in_dim(key_grads, key_term, block_index * tok_rows, 0)
        return (sum_now, key_grads)

    back_start = (zero_query, jnp.zeros((seq_rows, lat_width), jnp.float32))
    query_lat_grad, slot_key_grads = lax.fori_loop(0, slot_blocks, backward_loop, back_start)
    row_count = tok_rows * lax.axis_size("ctx")
    padding = jnp.zeros((row_count, lat_width), jnp.float32)
    padded = jnp.concatenate([padding, slot_key_grads, padding], axis=0)
    offset = jnp.clip(jnp.int32(0) - slot_start + row_count, 0, seq_rows + row_count)
    latent_grad = lax.psum_scatter(
        lax.dynamic_slice_in_dim(padded, offset, row_count, 0).astype(jnp.bfloat16),
        "ctx",
        scatter_dimension=0,
        tiled=True,
    )
    query_lat_low = query_lat_grad.reshape(NH, tok_rows, LAT).astype(jnp.bfloat16)
    key_up_grad = jnp.einsum(
        "shd,hsl->hdl",
        queries.reshape(tok_rows, NH, HD),
        query_lat_low,
        preferred_element_type=jnp.float32,
    ).reshape(NH * HD, LAT)
    query_grad = (
        jnp.einsum("hsl,hdl->shd", query_lat_low, key_heads, preferred_element_type=jnp.float32)
        .reshape(tok_rows, NH * HD)
        .astype(jnp.bfloat16)
    )
    query_w_grad = jnp.einsum("td,tk->dk", normed, query_grad, preferred_element_type=jnp.float32)
    latent_w_grad = jnp.einsum("td,tk->dk", normed, latent_grad, preferred_element_type=jnp.float32)
    normed_grad = jnp.einsum(
        "tk,dk->td", query_grad, query_full, preferred_element_type=jnp.float32
    ) + jnp.einsum("tk,dk->td", latent_grad, latent_full, preferred_element_type=jnp.float32)
    gain_one_grad = jnp.sum(normed_grad * normed_one, axis=0)
    input_grad = middle_grad + norm_back(normed_grad, normed_one, scale_one, gain_one_f)
    shards = (
        lax.psum_scatter(
            gain_one_grad.astype(jnp.bfloat16), "fsdp", scatter_dimension=0, tiled=True
        ).astype(jnp.float32),
        lax.psum_scatter(
            query_w_grad.astype(jnp.bfloat16), "fsdp", scatter_dimension=0, tiled=True
        ).astype(jnp.float32),
        lax.psum_scatter(
            latent_w_grad.astype(jnp.bfloat16), "fsdp", scatter_dimension=0, tiled=True
        ).astype(jnp.float32),
        lax.psum_scatter(
            key_up_grad.astype(jnp.bfloat16), "fsdp", scatter_dimension=0, tiled=True
        ).astype(jnp.float32),
        lax.psum_scatter(
            value_grad.astype(jnp.bfloat16), "fsdp", scatter_dimension=0, tiled=True
        ).astype(jnp.float32),
        lax.psum_scatter(
            output_grad.astype(jnp.bfloat16), "fsdp", scatter_dimension=0, tiled=True
        ).astype(jnp.float32),
        lax.psum_scatter(
            gain_two_grad.astype(jnp.bfloat16), "fsdp", scatter_dimension=0, tiled=True
        ).astype(jnp.float32),
        lax.psum_scatter(
            gate_w_grad.astype(jnp.bfloat16), "fsdp", scatter_dimension=1, tiled=True
        ).astype(jnp.float32),
        lax.psum_scatter(
            up_w_grad.astype(jnp.bfloat16), "fsdp", scatter_dimension=1, tiled=True
        ).astype(jnp.float32),
        lax.psum_scatter(
            down_grad.astype(jnp.bfloat16), "fsdp", scatter_dimension=0, tiled=True
        ).astype(jnp.float32),
    )
    summed = (
        lax.psum(shards[0].astype(jnp.bfloat16), "ctx").astype(jnp.float32),
        lax.psum(shards[1].astype(jnp.bfloat16), "ctx").astype(jnp.float32),
        lax.psum(shards[2].astype(jnp.bfloat16), "ctx").astype(jnp.float32),
        lax.psum(shards[3].astype(jnp.bfloat16), "ctx").astype(jnp.float32),
        lax.psum(shards[4].astype(jnp.bfloat16), "ctx").astype(jnp.float32),
        lax.psum(shards[5].astype(jnp.bfloat16), "ctx").astype(jnp.float32),
        lax.psum(shards[6].astype(jnp.bfloat16), "ctx").astype(jnp.float32),
        lax.psum(shards[7].astype(jnp.bfloat16), "ctx").astype(jnp.float32),
        lax.psum(shards[8].astype(jnp.bfloat16), "ctx").astype(jnp.float32),
        lax.psum(shards[9].astype(jnp.bfloat16), "ctx").astype(jnp.float32),
    )
    return (
        result[None],
        input_grad[None],
        summed[0],
        summed[1],
        summed[2],
        summed[3],
        summed[4],
        summed[5],
        summed[6],
        summed[7],
        summed[8],
        summed[9],
    )


def solution(mesh):
    return jax.shard_map(
        on_device,
        mesh=mesh,
        in_specs=(
            P("fsdp", "ctx", None),
            P("fsdp", "ctx", None),
            P("fsdp", None),
            P("fsdp"),
            P("fsdp", None),
            P("fsdp", None),
            P("fsdp", None),
            P("fsdp", None),
            P("fsdp", None),
            P("fsdp"),
            P(None, "fsdp"),
            P(None, "fsdp"),
            P("fsdp", None),
        ),
        out_specs=(
            P("fsdp", "ctx", None),
            P("fsdp", "ctx", None),
            P("fsdp"),
            P("fsdp", None),
            P("fsdp", None),
            P("fsdp", None),
            P("fsdp", None),
            P("fsdp", None),
            P("fsdp"),
            P(None, "fsdp"),
            P(None, "fsdp"),
            P("fsdp", None),
        ),
        check_vma=False,
    )
```

profile of v0, /device:TPU:0, one launch (start us, length us, event | category | flops | bytes accessed | tf_op | source)
XLA Modules:
  0.0 1036.9 jit_solution(728526672755502800)
XLA Ops:
  9.4 6.0 all-gather
  16.6 12.5 %all-gather.10.cloned.1.call-done = bf16[1024,512]{1,0:T(8,128)(2,1)} async-done(((bf16[256,512]{1,0:T(8,128)(2,1)}), bf16[1024,512]{1,0:T(8,128)(2,1)}) %all-gather.10.cloned.1.call-update) | async-done | bytes 1048592 | tf_op jit(solution)/shard_map/all_gather | solution.py:76
  29.0 2.6 convolution_convert_fusion.14
  34.9 5.1 all-gather.1
  40.0 10.9 %all_gather.38 = bf16[1024,256]{1,0:T(8,128)(2,1)} all-gather(bf16[256,256]{1,0:T(8,128)(2,1)S(1)} %copy-done.41), channel_id=1, replica_groups=mesh['ctx'=8,'fsdp'=4] {'fsdp'}, dimensions={0}, use_global_device_ids=true | all-gather | bytes 655360 | tf_op jit(solution)/shard_map/all_gather | solution.py:78
  50.9 7.3 all_gather.37
  58.2 2.5 convolution_convert_fusion.13
  60.9 2.1 convolution_convert_fusion.6
  63.0 2.9 copy.75
  65.9 42.2 %all-gather.12.cloned.1.call-done = bf16[2048,512]{1,0:T(8,128)(2,1)} async-done(((bf16[256,512]{1,0:T(8,128)(2,1)}), bf16[2048,512]{1,0:T(8,128)(2,1)}) %all-gather.12.cloned.1.call-update) | async-done | bytes 2097168 | tf_op jit(solution)/shard_map/all_gather | solution.py:140
  108.1 3.9 copy.70
  112.0 2.5 broadcast.245.clone
  114.5 10.8 %while.41 = (s32[]{:T(128)}, f32[2,8,256]{2,1,0:T(8,128)S(1)}, f32[2,8,256]{2,1,0:T(8,128)S(1)}, f32[2,8,256,256]{3,2,1,0:T(8,128)}, s32[]{:T(128)}, /*index=5*/...) while((s32[]{:T(128)}, f32[2,8,256]{2,1,0:T(8,128)S(1)}, ...), condition=%wide.region_6.7_spmd.clone, body=%wide.region_1.6_spmd.clone.sunk | while | flops 1089676544 | bytes 58203600 | solution.py:147
  114.5 10.4 %conditional.6 = ((f32[2,8,256]{2,1,0:T(8,128)S(1)}, f32[2,8,256]{2,1,0:T(8,128)S(1)}, f32[2,8,256,256]{3,2,1,0:T(8,128)})) conditional(s32[]{:T(128)} %convert_element_type.380, (f32[2,8,256]{2,1,0:T(8,128)S(1)}, f32[2,8,256]{2,1,0:T(8,128)S(1)}, f32[2,8,256,256]{3,2,1,0:T(8,128)}) %tuple.129, (s32[]{:T(128)}, s32[]{:T(128)}, s32[]{:T(128)}, ...), branch_computations={%region_2.2_spmd, %region_3.5_spmd} | conditional | flops 1089676544 | bytes 58202268 | solution.py:128
  115.8 2.8 fusion.4
  120.8 2.1 multiply_add_fusion
  122.9 2.0 copy-done.1
  125.2 5.9 copy.71
  131.1 2.7 fusion.44
  135.6 2.6 multiply_reduce_fusion.3
  139.3 36.1 %all-gather.18.cloned.1.call-done = bf16[1024,2816]{0,1:T(8,128)(2,1)} async-done(((bf16[1024,704]{0,1:T(8,128)(2,1)}), bf16[1024,2816]{0,1:T(8,128)(2,1)}) %all-gather.18.cloned.1.call-update) | async-done | bytes 5767184 | tf_op jit(solution)/shard_map/all_gather | solution.py:83
  175.4 5.9 fusion.79
  181.4 38.9 %all-gather.20.cloned.1.call-done = bf16[1024,2816]{0,1:T(8,128)(2,1)} async-done(((bf16[1024,704]{0,1:T(8,128)(2,1)}), bf16[1024,2816]{0,1:T(8,128)(2,1)}) %all-gather.20.cloned.1.call-update) | async-done | bytes 5767184 | tf_op jit(solution)/shard_map/all_gather | solution.py:84
  220.3 5.9 fusion.80
  226.2 39.1 %all-gather.22.cloned.1.call-done = bf16[2816,1024]{1,0:T(8,128)(2,1)} async-done(((bf16[704,1024]{1,0:T(8,128)(2,1)}), bf16[2816,1024]{1,0:T(8,128)(2,1)}) %all-gather.22.cloned.1.call-update) | async-done | bytes 5767184 | tf_op jit(solution)/shard_map/all_gather | solution.py:85
  265.3 8.2 multiply_convert_fusion
  273.5 5.4 fusion.81
  279.2 2.0 multiply_reduce_fusion.1
  284.7 2.0 copy.73
  288.6 3.7 multiply_reduce_fusion
  292.3 2.4 broadcast.245
  296.3 20.4 %while.42 = (s32[]{:T(128)}, f32[2,8,256,256]{3,2,1,0:T(8,128)}, bf16[2048,512]{0,1:T(8,128)(2,1)}, s32[]{:T(128)}, s32[]{:T(128)}, /*index=5*/s32[]{:T(128)}, s...) while((s32[]{:T(128)}, f32[2,8,256,256]{3,2,1,0:T(8,128)}, ...), condition=%wide.region_13.14_spmd.clone, body=%wide.region_10.13_spmd.clone.sunk | while | flops 2699625728 | bytes 97771040 | solution.py:246
  296.3 14.2 %conditional.7 = (f32[2,8,256,256]{3,2,1,0:T(8,128)}, bf16[256,512]{0,1:T(8,128)(2,1)S(1)}) conditional(s32[]{:T(128)} %convert_element_type.381, f32[2,8,256,256]{3,2,1,0:T(8,128)} %get-tuple-element.1157, (s32[]{:T(128)}, s32[]{:T(128)}, s32[]{:T(128)}, s32[]{:T(128)}, bf16[2048,512]{0,1:T(8,128)(2,1)}, ...), branch_computations={%region_11.11_spmd, %region_12.12_spmd} | conditional | flops 2699625728 | bytes 97245368 | solution.py:233
  297.5 2.8 fusion.78
  300.4 4.5 fusion.18
  318.3 4.3 fusion.42
  322.7 2.5 convert_element_type.249
  327.9 2.7 convolution_convert_fusion.9
  330.6 2.3 convolution_convert_fusion.11
  333.0 2.2 convolution_convert_fusion.4
  335.5 2.0 convolution_convert_fusion.3
  337.6 152.6 %reduce-scatter.10.cloned.1.call-done = bf16[256,512]{0,1:T(8,128)(2,1)} async-done(((bf16[2048,512]{0,1:T(8,128)(2,1)}), bf16[256,512]{0,1:T(8,128)(2,1)}) %reduce-scatter.10.cloned.1.call-update) | async-done | bytes 262160 | tf_op jit(solution)/shard_map/reduce_scatter | solution.py:251
  490.3 2.5 convolution_convert_fusion.7
  492.8 5.5 convolution_convert_fusion.2
  498.4 5.7 convolution_convert_fusion.1
  505.5 5.3 convolution_convert_fusion
  510.8 2.6 reduce-scatter.16.cloned.1.call-done
  513.4 24.2 %reduce-scatter.18.cloned.1.call-done = bf16[256,256]{1,0:T(8,128)(2,1)} async-done(((bf16[1024,256]{1,0:T(8,128)(2,1)}), bf16[256,256]{1,0:T(8,128)(2,1)}) %reduce-scatter.18.cloned.1.call-update) | async-done | bytes 131088 | tf_op jit(solution)/shard_map/reduce_scatter | solution.py:289
  537.6 34.6 %reduce-scatter.12.cloned.1.call-done = bf16[256,1024]{1,0:T(8,128)(2,1)} async-done(((bf16[1024,1024]{1,0:T(8,128)(2,1)}), bf16[256,1024]{1,0:T(8,128)(2,1)}) %reduce-scatter.12.cloned.1.call-update) | async-done | bytes 524304 | tf_op jit(solution)/shard_map/reduce_scatter | solution.py:280
  572.2 34.6 %reduce-scatter.20.cloned.1.call-done = bf16[256,1024]{1,0:T(8,128)(2,1)} async-done(((bf16[1024,1024]{1,0:T(8,128)(2,1)}), bf16[256,1024]{1,0:T(8,128)(2,1)}) %reduce-scatter.20.cloned.1.call-update) | async-done | bytes 524304 | tf_op jit(solution)/shard_map/reduce_scatter | solution.py:292
  606.8 28.0 %reduce-scatter.14.cloned.1.call-done = bf16[256,512]{1,0:T(8,128)(2,1)} async-done(((bf16[1024,512]{1,0:T(8,128)(2,1)}), bf16[256,512]{1,0:T(8,128)(2,1)}) %reduce-scatter.14.cloned.1.call-update) | async-done | bytes 262160 | tf_op jit(solution)/shard_map/reduce_scatter | solution.py:283
  634.8 57.5 %reduce-scatter.22.cloned.1.call-done = bf16[1024,704]{0,1:T(8,128)(2,1)} async-done(((bf16[1024,2816]{0,1:T(8,128)(2,1)}), bf16[1024,704]{0,1:T(8,128)(2,1)}) %reduce-scatter.22.cloned.1.call-update) | async-done | bytes 1441808 | tf_op jit(solution)/shard_map/reduce_scatter | solution.py:298
  692.3 57.3 %reduce-scatter.24.cloned.1.call-done = bf16[1024,704]{0,1:T(8,128)(2,1)} async-done(((bf16[1024,2816]{0,1:T(8,128)(2,1)}), bf16[1024,704]{0,1:T(8,128)(2,1)}) %reduce-scatter.24.cloned.1.call-update) | async-done | bytes 1441808 | tf_op jit(solution)/shard_map/reduce_scatter | solution.py:301
  749.6 57.5 %reduce-scatter.26.cloned.1.call-done = bf16[704,1024]{1,0:T(8,128)(2,1)} async-done(((bf16[2816,1024]{1,0:T(8,128)(2,1)}), bf16[704,1024]{1,0:T(8,128)(2,1)}) %reduce-scatter.26.cloned.1.call-update) | async-done | bytes 1441808 | tf_op jit(solution)/shard_map/reduce_scatter | solution.py:304
  808.9 2.5 fusion.82
  811.4 5.3 fusion.53
  817.5 6.1 all-reduce.4
  823.7 22.1 %all-reduce.2 = (bf16[256]{0:T(256)(128)(2,1)S(1)}, bf16[256]{0:T(256)(128)(2,1)S(1)}) all-reduce(bf16[256]{0:T(256)(128)(2,1)S(1)} %dynamic-slice.1, bf16[256]{0:T(256)(128)(2,1)S(1)} %dynamic-slice.3), channel_id=1, replica_groups=mesh['ctx'=8,'fsdp'=4] {'ctx'}, use_global_device_ids=true, to_apply=%region_18.19 | all-reduce | flops 512 | bytes 2048 | tf_op jit(solution)/shard_map/psum | solution.py:309
  848.2 167.7 %all-reduce.7.cloned.1.call-done = (bf16[256,1024]{1,0:T(8,128)(2,1)}, bf16[256,512]{1,0:T(8,128)(2,1)}, bf16[256,256]{1,0:T(8,128)(2,1)}, bf16[256,256]{1,0:T(8...) async-done(((bf16[256,1024]{1,0:T(8,128)(2,1)}, bf16[256,512]{1,0:T(8,128)(2,1)}, ...) | async-done | bytes 5898256 | tf_op jit(solution)/shard_map/psum | solution.py:310
  1015.9 2.3 convert_element_type.261
  1018.2 1.8 convert_element_type.263
  1024.3 1.9 convert_element_type.275
  1026.3 1.9 convert_element_type.277
  1028.2 1.9 convert_element_type.279
  (219 shorter events, 48.0 us)
Async XLA Ops:
  7.2 21.8 %all-gather.10.cloned.1.call-start = ((), (), s32[]{:S(2)}) async-start(), calls=%async_computation.9 | async-start | bytes 1310720 | tf_op jit(solution)/shard_map/all_gather | solution.py:76
  7.9 50.3 %all-gather.14.cloned.1.call-start = ((), (), s32[]{:S(2)}) async-start(), calls=%async_computation.11 | async-start | bytes 2621440 | tf_op jit(solution)/shard_map/all_gather | solution.py:75
  8.7 99.4 %all-gather.12.cloned.1.call-start = ((), (), s32[]{:S(2)}) async-start(), calls=%async_computation.10 | async-start | bytes 2359296 | tf_op jit(solution)/shard_map/all_gather | solution.py:140
  31.6 3.3 copy-start.44
  31.6 8.4 copy-start.41
  31.6 19.3 %copy-start.42 = (bf16[256,256]{1,0:T(8,128)(2,1)S(1)}, bf16[256,256]{1,0:T(8,128)(2,1)}, u32[]{:S(2)}) copy-start(bf16[256,256]{1,0:T(8,128)(2,1)} %param.27) | copy-start | bytes 393220
  31.6 104.0 %all-gather.16.cloned.1.call-start = ((), (), s32[]{:S(2)}) async-start(), calls=%async_computation.12 | async-start | bytes 2621440 | tf_op jit(solution)/shard_map/all_gather | solution.py:79
  32.2 26.0 %copy-start.8 = (bf16[1,256,1024]{2,1,0:T(8,128)(2,1)S(1)}, bf16[1,256,1024]{2,1,0:T(8,128)(2,1)}, u32[]{:S(2)}) copy-start(bf16[1,256,1024]{2,1,0:T(8,128)(2,1)} %param.21) | copy-start | bytes 1572868
  32.2 143.2 %all-gather.18.cloned.1.call-start = ((), (), s32[]{:S(2)}) async-start(), calls=%async_computation.13 | async-start | bytes 7208960 | tf_op jit(solution)/shard_map/all_gather | solution.py:83
  32.8 187.5 %all-gather.20.cloned.1.call-start = ((), (), s32[]{:S(2)}) async-start(), calls=%async_computation.14 | async-start | bytes 7208960 | tf_op jit(solution)/shard_map/all_gather | solution.py:84
  33.4 231.9 %all-gather.22.cloned.1.call-start = ((), (), s32[]{:S(2)}) async-start(), calls=%async_computation.15 | async-start | bytes 7208960 | tf_op jit(solution)/shard_map/all_gather | solution.py:85
  34.1 456.1 %reduce-scatter.10.cloned.1.call-start = ((), (), s32[]{:S(2)}) async-start(), calls=%async_computation.16 | async-start | bytes 2359296 | tf_op jit(solution)/shard_map/reduce_scatter | solution.py:251
  58.2 4.8 copy-start.22
  60.9 2.1 copy-start.28
  118.6 2.2 copy-start
  122.9 2.0 copy-start.1
  131.1 4.0 copy-start.24
  133.8 1.3 copy-start.5
  135.6 2.7 copy-start.20
  138.2 1.0 copy-start.11
  139.3 81.0 %copy-start.18 = (bf16[256,1024]{1,0:T(8,128)(2,1)}, bf16[256,1024]{1,0:T(8,128)(2,1)S(1)}, u32[]{:S(2)}) copy-start(bf16[256,1024]{1,0:T(8,128)(2,1)S(1)} %multiply_convert_fusion.3) | copy-start | bytes 1572868
  273.5 5.4 copy-start.34
  273.5 5.4 copy-start.33
  273.5 5.4 copy-start.12
  273.5 5.7 copy-start.43
  279.2 2.0 copy-start.32
  281.2 2.0 copy-start.14
  281.6 1.0 copy-start.9
  283.2 3.6 copy-start.25
  288.6 3.8 copy-start.15
  300.4 4.5 copy-start.2
  304.9 2.2 copy-start.4
  305.0 2.9 copy-start.16
  307.8 2.0 copy-start.3
  316.7 1.6 copy-start.17
  322.6 190.8 %reduce-scatter.16.cloned.1.call-start = ((), (), s32[]{:S(2)}) async-start(), calls=%async_computation.19 | async-start | bytes 655360 | tf_op jit(solution)/shard_map/reduce_scatter | solution.py:286
  322.7 3.8 copy-start.29
  325.2 1.3 copy-start.7
  325.2 2.7 copy-start.6
  327.8 2.8 copy-start.23
  327.8 209.8 %reduce-scatter.18.cloned.1.call-start = ((), (), s32[]{:S(2)}) async-start(), calls=%async_computation.20 | async-start | bytes 655360 | tf_op jit(solution)/shard_map/reduce_scatter | solution.py:289
  330.6 241.6 %reduce-scatter.12.cloned.1.call-start = ((), (), s32[]{:S(2)}) async-start(), calls=%async_computation.17 | async-start | bytes 2621440 | tf_op jit(solution)/shard_map/reduce_scatter | solution.py:280
  333.0 4.5 copy-start.26
  333.0 2.5 copy-start.10
  333.0 2.5 copy-start.21
  335.2 271.6 %reduce-scatter.20.cloned.1.call-start = ((), (), s32[]{:S(2)}) async-start(), calls=%async_computation.21 | async-start | bytes 2621440 | tf_op jit(solution)/shard_map/reduce_scatter | solution.py:292
  337.5 155.3 %copy-start.19 = (bf16[256,1024]{1,0:T(8,128)(2,1)S(1)}, bf16[256,1024]{1,0:T(8,128)(2,1)}, u32[]{:S(2)}) copy-start(bf16[256,1024]{1,0:T(8,128)(2,1)} %copy-done.18) | copy-start | bytes 1572868
  337.6 297.3 %reduce-scatter.14.cloned.1.call-start = ((), (), s32[]{:S(2)}) async-start(), calls=%async_computation.18 | async-start | bytes 1310720 | tf_op jit(solution)/shard_map/reduce_scatter | solution.py:283
  492.8 199.5 %reduce-scatter.22.cloned.1.call-start = ((), (), s32[]{:S(2)}) async-start(), calls=%async_computation.22 | async-start | bytes 7208960 | tf_op jit(solution)/shard_map/reduce_scatter | solution.py:298
  498.4 251.2 %reduce-scatter.24.cloned.1.call-start = ((), (), s32[]{:S(2)}) async-start(), calls=%async_computation.23 | async-start | bytes 7208960 | tf_op jit(solution)/shard_map/reduce_scatter | solution.py:301
  504.1 1.4 copy-start.30
  504.1 302.9 %reduce-scatter.26.cloned.1.call-start = ((), (), s32[]{:S(2)}) async-start(), calls=%async_computation.24 | async-start | bytes 7208960 | tf_op jit(solution)/shard_map/reduce_scatter | solution.py:304
  510.8 505.1 %all-reduce.7.cloned.1.call-start = ((), (), s32[]{:S(2)}) async-start(), calls=%async_computation.25 | async-start | bytes 11796480 | tf_op jit(solution)/shard_map/psum | solution.py:310
  807.0 0.7 copy-start.45
  807.0 1.9 copy-start.27
  807.1 4.3 copy-start.13
  808.9 2.5 copy-start.31
  811.4 5.3 copy-start.38
  811.4 5.3 copy-start.39
  1015.9 7.3 copy-start.40
  1015.9 8.4 copy-start.37
  1023.2 3.0 copy-start.36
  1026.3 1.9 copy-start.35
Sparse Core Ops, SparseCore 0:
  9.6 19.4 all-gather.9
  30.6 25.3 all-gather.13
  58.7 49.3 all-gather.11
  109.5 21.0 all-gather.15
  132.0 43.3 all-gather.17
  176.9 43.3 all-gather.19
  221.9 43.3 all-gather.21
  322.7 167.4 reduce-scatter.9
  492.7 20.6 reduce-scatter.15
  515.9 21.6 reduce-scatter.17
  540.7 31.4 reduce-scatter.11
  575.3 31.4 reduce-scatter.19
  609.9 24.8 reduce-scatter.13
  637.4 54.8 reduce-scatter.21
  694.7 54.8 reduce-scatter.23
  752.1 54.8 reduce-scatter.25
  811.5 204.3 all-reduce.6
where the time goes:
time: 1050 us; the launch traced here: 1040 us
  waiting for transfers between devices  789 us (75%)
  matrix products  94.2 us (9%)
  blocking collectives  57.4 us (5%)
  local copies, waits for them, and re-layouts  45.5 us (4%)
  other arithmetic  33 us (3%)
  between operations  16 us (2%)
    psum x1, waiting for transfers between devices, on_device(): lax.psum(shards[1].astype(jnp.bfloat16), 'ctx').astype(jnp.float32)  168 us
    reduce_scatter x1, waiting for transfers between devices, on_device(): lax.psum_scatter(lax.dynamic_slice_in_dim(padded, offset, row_count, 0).a...  153 us
    reduce_scatter x1, waiting for transfers between devices, on_device(): lax.psum_scatter(gate_w_grad.astype(jnp.bfloat16), 'fsdp', scatter_dimens...  57.5 us
    reduce_scatter x1, waiting for transfers between devices, on_device(): lax.psum_scatter(down_grad.astype(jnp.bfloat16), 'fsdp', scatter_dimensio...  57.5 us
    reduce_scatter x1, waiting for transfers between devices, on_device(): lax.psum_scatter(up_w_grad.astype(jnp.bfloat16), 'fsdp', scatter_dimensio...  57.3 us
    all_gather x1, waiting for transfers between devices, on_device(): group_latent = lax.all_gather(latent, 'ctx', axis=0, tiled=True)  42.2 us
    all_gather x1, waiting for transfers between devices, on_device(): lax.all_gather(w_down, 'fsdp', axis=0, tiled=True)  39.1 us
    all_gather x1, waiting for transfers between devices, on_device(): lax.all_gather(w_up, 'fsdp', axis=1, tiled=True)  38.9 us
  transfers between devices with their start and end apart: 17, of which 15 were waited for; matrix products, arithmetic and copies ran while one was open for 9% of the time, Pallas kernels for 0%

commit v1 on v0

--- a/solution.py
+++ b/solution.py
@@ -10,6 +10,19 @@
 SEQ_MAX = 4096
 EPS = 1e-06
 NEGATIVE = -1e30
+
+
+def ring_gather(value, axis, dim):
+    size, index, rows = (lax.axis_size(axis), lax.axis_index(axis), value.shape[dim])
+    right = [(i, (i + 1) % size) for i in range(size)]
+    out = jnp.zeros((*value.shape[:dim], size * rows, *value.shape[dim + 1 :]), value.dtype)
+    block = value
+    for lap in range(size):
+        holder = (index - lap) % size
+        out = lax.dynamic_update_slice_in_dim(out, block, holder * rows, axis=dim)
+        if lap < size - 1:
+            block = lax.ppermute(block, axis, right)
+    return out
 
 
 def norm_scale(values):
@@ -82,7 +95,7 @@
         lax.all_gather(norm2_gain, "fsdp", axis=0, tiled=True),
         lax.all_gather(w_gate, "fsdp", axis=1, tiled=True),
         lax.all_gather(w_up, "fsdp", axis=1, tiled=True),
-        lax.all_gather(w_down, "fsdp", axis=0, tiled=True),
+        ring_gather(w_down, "fsdp", 0),
     )
     gain_one_f = gain_one.astype(jnp.float32)
     gain_two_f = gain_two.astype(jnp.float32)

time: 1050 us -> 992 us (0.945)
  waiting for transfers between devices: 789 us -> 716 us
  blocking collectives: 57.4 us -> 77.9 us
  local copies, waits for them, and re-layouts: 45.5 us -> 61.1 us
  matrix products: 94.2 us -> 81.9 us
    all_gather x1, waiting for transfers between devices: 42.2 us -> 0.01 us  [on_device(): group_latent = lax.all_gather(latent, 'ctx', axis=0, tiled=True)]
    all_gather x1 -> x0, waiting for transfers between devices: 39.1 us -> none  [on_device(): lax.all_gather(w_down, 'fsdp', axis=0, tiled=True)]
    ppermute x0 -> x3, waiting for transfers between devices: none -> 29.4 us  [ring_gather(): block = lax.ppermute(block, axis, right)]
    reduce_scatter x1, waiting for transfers between devices: 2.6 us -> 24.9 us  [on_device(): lax.psum_scatter(key_up_grad.astype(jnp.bfloat16), 'fsdp', scatter_dimens...]
    reduce_scatter x1, waiting for transfers between devices: 24.2 us -> 4.89 us  [on_device(): lax.psum_scatter(value_grad.astype(jnp.bfloat16), 'fsdp', scatter_dimensi...]
    all_gather x1, waiting for transfers between devices: 36.1 us -> 18.2 us  [on_device(): lax.all_gather(w_gate, 'fsdp', axis=1, tiled=True)]
    all_gather x1, blocking collectives: 5.07 us -> 18.6 us  [on_device(): lax.all_gather(norm2_gain, 'fsdp', axis=0, tiled=True)]
  transfers between devices with their start and end apart: 17 -> 19, of which waited for: 15 -> 14; matrix products, arithmetic and copies ran while one was open for 9% -> 10% of each run, Pallas kernels for 0% -> 0%
where the time goes in v1:
time: 992 us; the launch traced here: 986 us
  waiting for transfers between devices  716 us (72%)
  matrix products  81.9 us (8%)
  blocking collectives  77.9 us (8%)
  local copies, waits for them, and re-layouts  61.1 us (6%)
  other arithmetic  30.4 us (3%)
  between operations  16.1 us (2%)
    psum x1, waiting for transfers between devices, on_device(): lax.psum(shards[1].astype(jnp.bfloat16), 'ctx').astype(jnp.float32)  168 us
    reduce_scatter x1, waiting for transfers between devices, on_device(): lax.psum_scatter(lax.dynamic_slice_in_dim(padded, offset, row_count, 0).a...  147 us
    reduce_scatter x1, waiting for transfers between devices, on_device(): lax.psum_scatter(gate_w_grad.astype(jnp.bfloat16), 'fsdp', scatter_dimens...  57.6 us
    reduce_scatter x1, waiting for transfers between devices, on_device(): lax.psum_scatter(down_grad.astype(jnp.bfloat16), 'fsdp', scatter_dimensio...  57.5 us
    reduce_scatter x1, waiting for transfers between devices, on_device(): lax.psum_scatter(up_w_grad.astype(jnp.bfloat16), 'fsdp', scatter_dimensio...  57.3 us
    all_gather x1, waiting for transfers between devices, on_device(): lax.all_gather(w_up, 'fsdp', axis=1, tiled=True)  38.9 us
    reduce_scatter x1, waiting for transfers between devices, on_device(): lax.psum_scatter(query_w_grad.astype(jnp.bfloat16), 'fsdp', scatter_dimen...  34.7 us
    reduce_scatter x1, waiting for transfers between devices, on_device(): lax.psum_scatter(output_grad.astype(jnp.bfloat16), 'fsdp', scatter_dimens...  34.4 us
  transfers between devices with their start and end apart: 19, of which 14 were waited for; matrix products, arithmetic and copies ran while one was open for 10% of the time, Pallas kernels for 0%

profile of v1, /device:TPU:0, one launch (start us, length us, event | category | flops | bytes accessed | tf_op | source)
XLA Modules:
  0.0 985.7 jit_solution(1505287876093324529)
XLA Ops:
  9.4 6.0 all-gather
  16.6 12.4 %all-gather.9.cloned.1.call-done = bf16[1024,512]{1,0:T(8,128)(2,1)} async-done(((bf16[256,512]{1,0:T(8,128)(2,1)}), bf16[1024,512]{1,0:T(8,128)(2,1)}) %all-gather.9.cloned.1.call-update) | async-done | bytes 1048592 | tf_op jit(solution)/shard_map/all_gather | solution.py:89
  29.0 2.7 convolution_convert_fusion.14
  33.8 29.4 %collective-permute-done = bf16[704,1024]{1,0:T(8,128)(2,1)S(1)} collective-permute-done((bf16[704,1024]{1,0:T(8,128)(2,1)S(1)}, bf16[704,1024]{1,0:T(8,128)(2,1)S(1)}, u32[]{:S(2)}, u32[]{:S(2)}) %collective-permute-start) | collective-permute-done | bytes 1441824 | tf_op jit(solution)/shard_map/ppermute | solution.py:24
  64.0 18.6 %all-gather.1 = bf16[4,1,256]{2,1,0:T(2,128)(2,1)S(1)} all-gather(bf16[1,1,256]{2,1,0:T(2,128)(2,1)S(1)} %reshape.281), channel_id=1, replica_groups=mesh['ctx'=8,'fsdp'=4] {'fsdp'}, dimensions={0}, use_global_device_ids=true | all-gather | bytes 2560 | tf_op jit(solution)/shard_map/all_gather | solution.py:95
  82.8 3.2 broadcast_in_dim.88
  87.3 17.7 %all_gather.34 = bf16[1024,256]{1,0:T(8,128)(2,1)S(1)} all-gather(bf16[256,256]{1,0:T(8,128)(2,1)S(1)} %copy-done.39), channel_id=1, replica_groups=mesh['ctx'=8,'fsdp'=4] {'fsdp'}, dimensions={0}, use_global_device_ids=true | all-gather | bytes 655360 | tf_op jit(solution)/shard_map/all_gather | solution.py:90
  104.9 7.5 all_gather.35
  112.5 2.7 constant_dynamic-update-slice_fusion.3
  115.1 2.6 constant_dynamic-update-slice_fusion.2
  117.8 2.7 convolution_convert_fusion.13
  120.7 2.1 convolution_convert_fusion.6
  122.8 3.4 copy.75
  126.1 2.6 constant_dynamic-update-slice_fusion.1
  128.7 3.9 copy.70
  132.6 2.5 broadcast.249.clone
  135.2 11.2 %while.41 = (s32[]{:T(128)}, f32[2,8,256]{2,1,0:T(8,128)S(1)}, f32[2,8,256]{2,1,0:T(8,128)S(1)}, f32[2,8,256,256]{3,2,1,0:T(8,128)}, s32[]{:T(128)}, /*index=5*/...) while((s32[]{:T(128)}, f32[2,8,256]{2,1,0:T(8,128)S(1)}, ...), condition=%wide.region_6.7_spmd.clone, body=%wide.region_1.0_spmd.clone.sunk | while | flops 1089676544 | bytes 58203592 | solution.py:160
  135.2 10.8 %conditional.6 = ((f32[2,8,256]{2,1,0:T(8,128)S(1)}, f32[2,8,256]{2,1,0:T(8,128)S(1)}, f32[2,8,256,256]{3,2,1,0:T(8,128)})) conditional(s32[]{:T(128)} %convert_element_type.380, (f32[2,8,256]{2,1,0:T(8,128)S(1)}, f32[2,8,256]{2,1,0:T(8,128)S(1)}, f32[2,8,256,256]{3,2,1,0:T(8,128)}) %tuple.129, (s32[]{:T(128)}, s32[]{:T(128)}, s32[]{:T(128)}, ...), branch_computations={%region_2.2_spmd, %region_3.5_spmd} | conditional | flops 1089676544 | bytes 58202268 | solution.py:141
  136.6 2.7 fusion.4
  141.8 2.1 multiply_add_fusion
  143.9 2.1 copy-done.1
  146.4 5.4 copy.71
  151.8 2.7 fusion.44
  156.4 2.6 multiply_reduce_fusion.3
  160.1 18.2 %all-gather.17.cloned.1.call-done = bf16[1024,2816]{0,1:T(8,128)(2,1)} async-done(((bf16[1024,704]{0,1:T(8,128)(2,1)}), bf16[1024,2816]{0,1:T(8,128)(2,1)}) %all-gather.17.cloned.1.call-update) | async-done | bytes 5767184 | tf_op jit(solution)/shard_map/all_gather | solution.py:96
  178.3 5.9 fusion.79
  184.2 38.9 %all-gather.19.cloned.1.call-done = bf16[1024,2816]{0,1:T(8,128)(2,1)} async-done(((bf16[1024,704]{0,1:T(8,128)(2,1)}), bf16[1024,2816]{0,1:T(8,128)(2,1)}) %all-gather.19.cloned.1.call-update) | async-done | bytes 5767184 | tf_op jit(solution)/shard_map/all_gather | solution.py:97
  223.1 4.5 fusion.80
  227.7 8.8 multiply_convert_fusion
  238.5 1.9 multiply_reduce_fusion.1
  243.9 2.0 copy.73
  246.0 1.9 convolution_convert_fusion.5
  247.9 3.6 multiply_reduce_fusion
  251.5 2.4 broadcast.249
  255.5 17.4 %while.42 = (s32[]{:T(128)}, f32[2,8,256,256]{3,2,1,0:T(8,128)}, bf16[2048,512]{0,1:T(8,128)(2,1)}, s32[]{:T(128)}, s32[]{:T(128)}, /*index=5*/s32[]{:T(128)}, s...) while((s32[]{:T(128)}, f32[2,8,256,256]{3,2,1,0:T(8,128)}, ...), condition=%wide.region_13.14_spmd.clone, body=%wide.region_10.13_spmd.clone.sunk | while | flops 2699625728 | bytes 80993792 | solution.py:259
  255.5 11.1 %conditional.7 = (f32[2,8,256,256]{3,2,1,0:T(8,128)}, bf16[256,512]{0,1:T(8,128)(2,1)S(1)}) conditional(s32[]{:T(128)} %convert_element_type.381, f32[2,8,256,256]{3,2,1,0:T(8,128)} %get-tuple-element.1157, (s32[]{:T(128)}, s32[]{:T(128)}, s32[]{:T(128)}, s32[]{:T(128)}, bf16[2048,512]{0,1:T(8,128)(2,1)}, ...), branch_computations={%region_11.11_spmd, %region_12.12_spmd} | conditional | flops 2699625728 | bytes 80468128 | solution.py:246
  264.6 2.0 copy-done.3
  274.5 4.3 fusion.42
  278.9 2.6 convolution_convert_fusion.9
  281.6 2.5 convert_element_type.249
  285.5 3.4 convolution_convert_fusion.3
  289.0 1.8 convolution_convert_fusion.11
  291.6 2.2 convolution_convert_fusion.4
  293.8 146.8 %reduce-scatter.10.cloned.1.call-done = bf16[256,512]{0,1:T(8,128)(2,1)} async-done(((bf16[2048,512]{0,1:T(8,128)(2,1)}), bf16[256,512]{0,1:T(8,128)(2,1)}) %reduce-scatter.10.cloned.1.call-update) | async-done | bytes 262160 | tf_op jit(solution)/shard_map/reduce_scatter | solution.py:264
  440.6 2.5 convolution_convert_fusion.7
  443.2 4.2 convolution_convert_fusion.2
  448.7 4.2 convolution_convert_fusion.1
  454.4 4.2 convolution_convert_fusion
  458.9 4.9 reduce-scatter.18.cloned.1.call-done
  463.8 24.9 %reduce-scatter.16.cloned.1.call-done = bf16[256,256]{1,0:T(8,128)(2,1)} async-done(((bf16[1024,256]{1,0:T(8,128)(2,1)}), bf16[256,256]{1,0:T(8,128)(2,1)}) %reduce-scatter.16.cloned.1.call-update) | async-done | bytes 131088 | tf_op jit(solution)/shard_map/reduce_scatter | solution.py:299
  488.7 34.4 %reduce-scatter.20.cloned.1.call-done = bf16[256,1024]{1,0:T(8,128)(2,1)} async-done(((bf16[1024,1024]{1,0:T(8,128)(2,1)}), bf16[256,1024]{1,0:T(8,128)(2,1)}) %reduce-scatter.20.cloned.1.call-update) | async-done | bytes 524304 | tf_op jit(solution)/shard_map/reduce_scatter | solution.py:305
  523.1 34.7 %reduce-scatter.12.cloned.1.call-done = bf16[256,1024]{1,0:T(8,128)(2,1)} async-done(((bf16[1024,1024]{1,0:T(8,128)(2,1)}), bf16[256,1024]{1,0:T(8,128)(2,1)}) %reduce-scatter.12.cloned.1.call-update) | async-done | bytes 524304 | tf_op jit(solution)/shard_map/reduce_scatter | solution.py:293
  557.9 27.9 %reduce-scatter.14.cloned.1.call-done = bf16[256,512]{1,0:T(8,128)(2,1)} async-done(((bf16[1024,512]{1,0:T(8,128)(2,1)}), bf16[256,512]{1,0:T(8,128)(2,1)}) %reduce-scatter.14.cloned.1.call-update) | async-done | bytes 262160 | tf_op jit(solution)/shard_map/reduce_scatter | solution.py:296
  585.8 57.6 %reduce-scatter.22.cloned.1.call-done = bf16[1024,704]{0,1:T(8,128)(2,1)} async-done(((bf16[1024,2816]{0,1:T(8,128)(2,1)}), bf16[1024,704]{0,1:T(8,128)(2,1)}) %reduce-scatter.22.cloned.1.call-update) | async-done | bytes 1441808 | tf_op jit(solution)/shard_map/reduce_scatter | solution.py:311
  643.4 57.3 %reduce-scatter.24.cloned.1.call-done = bf16[1024,704]{0,1:T(8,128)(2,1)} async-done(((bf16[1024,2816]{0,1:T(8,128)(2,1)}), bf16[1024,704]{0,1:T(8,128)(2,1)}) %reduce-scatter.24.cloned.1.call-update) | async-done | bytes 1441808 | tf_op jit(solution)/shard_map/reduce_scatter | solution.py:314
  700.6 57.5 %reduce-scatter.26.cloned.1.call-done = bf16[704,1024]{1,0:T(8,128)(2,1)} async-done(((bf16[2816,1024]{1,0:T(8,128)(2,1)}), bf16[704,1024]{1,0:T(8,128)(2,1)}) %reduce-scatter.26.cloned.1.call-update) | async-done | bytes 1441808 | tf_op jit(solution)/shard_map/reduce_scatter | solution.py:317
  760.0 2.3 fusion.82
  762.4 5.6 fusion.53
  768.8 6.1 all-reduce.4
  775.0 22.1 %all-reduce.2 = (bf16[256]{0:T(256)(128)(2,1)S(1)}, bf16[256]{0:T(256)(128)(2,1)S(1)}) all-reduce(bf16[256]{0:T(256)(128)(2,1)S(1)} %dynamic-slice.1, bf16[256]{0:T(256)(128)(2,1)S(1)} %dynamic-slice.3), channel_id=1, replica_groups=mesh['ctx'=8,'fsdp'=4] {'ctx'}, use_global_device_ids=true, to_apply=%region_18.19 | all-reduce | flops 512 | bytes 2048 | tf_op jit(solution)/shard_map/psum | solution.py:322
  799.5 167.7 %all-reduce.7.cloned.1.call-done = (bf16[256,1024]{1,0:T(8,128)(2,1)}, bf16[256,512]{1,0:T(8,128)(2,1)}, bf16[256,256]{1,0:T(8,128)(2,1)}, bf16[256,256]{1,0:T(8...) async-done(((bf16[256,1024]{1,0:T(8,128)(2,1)}, bf16[256,512]{1,0:T(8,128)(2,1)}, ...) | async-done | bytes 5898256 | tf_op jit(solution)/shard_map/psum | solution.py:323
  967.2 3.4 convert_element_type.275
  970.6 1.9 convert_element_type.277
  972.5 1.9 convert_element_type.279
  (243 shorter events, 52.4 us)
Async XLA Ops:
  7.2 21.8 %all-gather.9.cloned.1.call-start = ((), (), s32[]{:S(2)}) async-start(), calls=%async_computation.9 | async-start | bytes 1310720 | tf_op jit(solution)/shard_map/all_gather | solution.py:89
  7.9 109.8 %all-gather.13.cloned.1.call-start = ((), (), s32[]{:S(2)}) async-start(), calls=%async_computation.11 | async-start | bytes 2621440 | tf_op jit(solution)/shard_map/all_gather | solution.py:88
  8.7 120.1 %all-gather.11.cloned.1.call-start = ((), (), s32[]{:S(2)}) async-start(), calls=%async_computation.10 | async-start | bytes 2359296 | tf_op jit(solution)/shard_map/all_gather | solution.py:153
  15.3 102.4 %copy-start.43 = (f32[4,1,256]{2,1,0:T(1,128)}, f32[4,1,256]{2,1,0:T(1,128)S(1)}, u32[]{:S(2)}) copy-start(f32[4,1,256]{2,1,0:T(1,128)S(1)} %convert_element_type.282) | copy-start | bytes 12292
  16.6 101.2 %copy-start.45 = (f32[256]{0:T(256)}, f32[256]{0:T(256)S(1)}, u32[]{:S(2)}) copy-start(f32[256]{0:T(256)S(1)} %add_rsqrt_fusion.1) | copy-start | bytes 3076
  29.0 4.5 copy-start.30
  29.0 34.9 %copy-start.47 = (bf16[256]{0:T(256)(128)(2,1)S(1)}, bf16[256]{0:T(256)(128)(2,1)}, u32[]{:S(2)}) copy-start(bf16[256]{0:T(256)(128)(2,1)} %param.30) | copy-start | bytes 1540
  31.7 124.6 %all-gather.15.cloned.1.call-start = ((), (), s32[]{:S(2)}) async-start(), calls=%async_computation.12 | async-start | bytes 2621440 | tf_op jit(solution)/shard_map/all_gather | solution.py:92
  32.3 146.0 %all-gather.17.cloned.1.call-start = ((), (), s32[]{:S(2)}) async-start(), calls=%async_computation.13 | async-start | bytes 7208960 | tf_op jit(solution)/shard_map/all_gather | solution.py:96
  32.9 190.2 %all-gather.19.cloned.1.call-start = ((), (), s32[]{:S(2)}) async-start(), calls=%async_computation.14 | async-start | bytes 7208960 | tf_op jit(solution)/shard_map/all_gather | solution.py:97
  33.5 407.1 %reduce-scatter.10.cloned.1.call-start = ((), (), s32[]{:S(2)}) async-start(), calls=%async_computation.15 | async-start | bytes 2359296 | tf_op jit(solution)/shard_map/reduce_scatter | solution.py:264
  33.5 29.7 %collective-permute-start = (bf16[704,1024]{1,0:T(8,128)(2,1)S(1)}, bf16[704,1024]{1,0:T(8,128)(2,1)S(1)}, u32[]{:S(2)}, u32[]{:S(2)}) collective-permute-start(bf16[704,1024]{1,0:T(8,128)(2,1)S(1)} %copy-done.30), channel_id=1, source_target_pairs={{0,1},{1,2},{2,3},{3,0},{4,5},{5,6},{6,7},{7,4},{8,9},{9,10},{10,1... | collective-permute-start | bytes 4325384 | tf_op jit(solution)/shard_map/ppermute | solution.py:24
  63.3 22.8 %copy-start.31 = (bf16[704,1024]{1,0:T(8,128)(2,1)}, bf16[704,1024]{1,0:T(8,128)(2,1)S(1)}, u32[]{:S(2)}) copy-start(bf16[704,1024]{1,0:T(8,128)(2,1)S(1)} %collective-permute-done) | copy-start | bytes 4325380
  63.3 19.3 %collective-permute-start.1 = (bf16[704,1024]{1,0:T(8,128)(2,1)S(1)}, bf16[704,1024]{1,0:T(8,128)(2,1)}, u32[]{:S(2)}, u32[]{:S(2)}) collective-permute-start(bf16[704,1024]{1,0:T(8,128)(2,1)S(1)} %collective-permute-done), channel_id=1, source_target_pairs={{0,1},{1,2},{2,3},{3,0},{4,5},{5,6},{6,7},{7,4},{8,9},{9,10},{10,1... | collective-permute-start | bytes 4325384 | tf_op jit(solution)/shard_map/ppermute | solution.py:24
  82.6 43.5 %collective-permute-start.2 = (bf16[704,1024]{1,0:T(8,128)(2,1)}, bf16[704,1024]{1,0:T(8,128)(2,1)}, u32[]{:S(2)}, u32[]{:S(2)}) collective-permute-start(bf16[704,1024]{1,0:T(8,128)(2,1)} %collective-permute-done.1), channel_id=1, source_target_pairs={{0,1},{1,2},{2,3},{3,0},{4,5},{5,6},{6,7},{7,4},{8,9},{9,10},{10,1... | collective-permute-start | bytes 4325384 | tf_op jit(solution)/shard_map/ppermute | solution.py:24
  86.1 18.9 %copy-start.40 = (bf16[256,256]{1,0:T(8,128)(2,1)S(1)}, bf16[256,256]{1,0:T(8,128)(2,1)}, u32[]{:S(2)}) copy-start(bf16[256,256]{1,0:T(8,128)(2,1)} %param.28) | copy-start | bytes 393220
  104.9 15.7 %copy-start.17 = (bf16[1024,256]{1,0:T(8,128)(2,1)}, bf16[1024,256]{1,0:T(8,128)(2,1)S(1)}, u32[]{:S(2)}) copy-start(bf16[1024,256]{1,0:T(8,128)(2,1)S(1)} %all_gather.34) | copy-start | bytes 1572868
  112.5 5.3 copy-start.6
  120.7 2.1 copy-start.21
  139.3 2.5 copy-start
  143.9 2.1 copy-start.1
  151.8 4.1 copy-start.18
  156.3 2.7 copy-start.16
  223.1 4.5 copy-start.24
  223.1 13.3 %slice-start = ((s8[5767168]{0:T(1024)(128)(4,1)}), s8[4194304]{0:T(1024)(128)(4,1)S(1)}, s32[]{:S(2)}) async-start(s8[5767168]{0:T(1024)(128)(4,1)} %bitcast.218), calls=%async_computation.25 | async-start | bytes 8388608
  223.1 15.0 %slice-start.2 = ((s8[5767168]{0:T(1024)(128)(4,1)}), s8[4194304]{0:T(1024)(128)(4,1)S(1)}, s32[]{:S(2)}) async-start(s8[5767168]{0:T(1024)(128)(4,1)} %bitcast.220), calls=%async_computation.27 | async-start | bytes 8388608
  227.6 8.8 slice-start.1
  227.7 10.5 %slice-start.3 = ((s8[5767168]{0:T(1024)(128)(4,1)}), s8[1572864]{0:T(1024)(128)(4,1)S(1)}, s32[]{:S(2)}) async-start(s8[5767168]{0:T(1024)(128)(4,1)} %bitcast.220), calls=%async_computation.28 | async-start | bytes 3145728
  236.4 1.7 copy-start.28
  236.4 1.7 copy-start.26
  236.5 2.0 copy-start.10
  240.4 2.0 copy-start.12
  247.9 3.6 copy-start.13
  256.9 1.6 copy-start.14
  261.2 2.2 copy-start.2
  264.6 2.0 copy-start.3
  272.9 1.6 copy-start.15
  274.5 4.3 copy-start.5
  278.8 185.0 %reduce-scatter.18.cloned.1.call-start = ((), (), s32[]{:S(2)}) async-start(), calls=%async_computation.19 | async-start | bytes 655360 | tf_op jit(solution)/shard_map/reduce_scatter | solution.py:302
  281.5 207.2 %reduce-scatter.16.cloned.1.call-start = ((), (), s32[]{:S(2)}) async-start(), calls=%async_computation.18 | async-start | bytes 655360 | tf_op jit(solution)/shard_map/reduce_scatter | solution.py:299
  281.6 2.5 copy-start.22
  285.4 237.7 %reduce-scatter.20.cloned.1.call-start = ((), (), s32[]{:S(2)}) async-start(), calls=%async_computation.20 | async-start | bytes 2621440 | tf_op jit(solution)/shard_map/reduce_scatter | solution.py:305
  288.9 2.7 copy-start.44
  288.9 2.7 copy-start.46
  288.9 269.0 %reduce-scatter.12.cloned.1.call-start = ((), (), s32[]{:S(2)}) async-start(), calls=%async_computation.16 | async-start | bytes 2621440 | tf_op jit(solution)/shard_map/reduce_scatter | solution.py:293
  293.7 149.5 %copy-start.29 = (bf16[256,2816]{1,0:T(8,128)(2,1)S(1)}, bf16[256,2816]{1,0:T(8,128)(2,1)}, u32[]{:S(2)}) copy-start(bf16[256,2816]{1,0:T(8,128)(2,1)} %copy-done.28) | copy-start | bytes 4325380
  293.8 292.0 %reduce-scatter.14.cloned.1.call-start = ((), (), s32[]{:S(2)}) async-start(), calls=%async_computation.17 | async-start | bytes 1310720 | tf_op jit(solution)/shard_map/reduce_scatter | solution.py:296
  443.1 200.2 %reduce-scatter.22.cloned.1.call-start = ((), (), s32[]{:S(2)}) async-start(), calls=%async_computation.21 | async-start | bytes 7208960 | tf_op jit(solution)/shard_map/reduce_scatter | solution.py:311
  447.4 253.2 %reduce-scatter.24.cloned.1.call-start = ((), (), s32[]{:S(2)}) async-start(), calls=%async_computation.22 | async-start | bytes 7208960 | tf_op jit(solution)/shard_map/reduce_scatter | solution.py:314
  452.9 1.5 copy-start.25
  452.9 305.2 %reduce-scatter.26.cloned.1.call-start = ((), (), s32[]{:S(2)}) async-start(), calls=%async_computation.23 | async-start | bytes 7208960 | tf_op jit(solution)/shard_map/reduce_scatter | solution.py:317
  458.6 508.6 %all-reduce.7.cloned.1.call-start = ((), (), s32[]{:S(2)}) async-start(), calls=%async_computation.24 | async-start | bytes 11796480 | tf_op jit(solution)/shard_map/psum | solution.py:323
  758.1 1.9 copy-start.20
  758.2 4.2 copy-start.11
  762.4 5.6 copy-start.34
  762.4 5.6 copy-start.35
  768.0 30.2 %copy-start.8 = (f32[256,1024]{1,0:T(8,128)S(1)}, f32[256,1024]{1,0:T(8,128)}, u32[]{:S(2)}) copy-start(f32[256,1024]{1,0:T(8,128)} %copy-done.7) | copy-start | bytes 3145732
  967.2 3.4 copy-start.33
  970.6 1.9 copy-start.32
  972.5 2.0 copy-start.37
  972.5 3.0 copy-start.36
  972.5 4.1 copy-start.38
  974.5 3.0 copy-start.42
  974.5 3.8 copy-start.41
  (8 other events, 8.7 us)
Sparse Core Ops, SparseCore 0:
  9.6 19.4 all-gather.8
  30.6 28.2 all-gather.12
  61.6 49.2 all-gather.10
  112.3 21.0 all-gather.14
  134.8 43.3 all-gather.16
  179.7 43.3 all-gather.18
  278.9 161.6 reduce-scatter.9
  443.1 20.6 reduce-scatter.17
  467.0 21.6 reduce-scatter.15
  491.7 31.4 reduce-scatter.19
  526.4 31.4 reduce-scatter.11
  560.8 24.8 reduce-scatter.13
  588.5 54.8 reduce-scatter.21
  645.8 54.8 reduce-scatter.23
  703.2 54.8 reduce-scatter.25
  762.6 204.5 all-reduce.6
